TPU v7x, 32 devices: a whole 2x2x4 slice. The times are simulated.
32 devices in a mesh: dp: 4 (over z), mp: 8 (over y, x, core).
Axes of the slice: x: 2, y: 2, z: 4, core: 2. Of those that a mesh axis runs over, the one named last changes fastest.
Arguments:
- activations: bfloat16 [1024, 12288], P('dp', 'mp'), may hold values from -6 to 6
- out_grad: bfloat16 [1024, 12288], P('dp', 'mp'), may hold values from -1.5 to 1.5
- up_blocks: bfloat16 [128, 4224, 128], P(None, 'mp'), may hold values from -0.15625 to 0.15625
- down_blocks: bfloat16 [128, 4224, 128], P(None, 'mp'), may hold values from -0.078125 to 0.078125
- latent_in: bfloat16 [256, 12288], P(None, 'mp'), may hold values from -0.0546875 to 0.0546875
- latent_out: bfloat16 [256, 49152], P(None, 'mp'), may hold values from -0.375 to 0.375
- block_rows: int32 [11, 384], P(None, 'mp'), may hold values from 0 to 95, as said below
- section_count: int32 [384], P('mp'), may hold values from 1 to 11, as said below
Outputs:
- mixed: bfloat16 [1024, 12288], P('dp', 'mp')
- input_grad: bfloat16 [1024, 12288], P('dp', 'mp')
- up_grad: bfloat16 [128, 4224, 128], P('dp', 'mp')
- down_grad: bfloat16 [128, 4224, 128], P('dp', 'mp')
- latent_in_grad: bfloat16 [256, 12288], P('dp', 'mp')
- latent_out_grad: bfloat16 [256, 49152], P('dp', 'mp')
Inputs may be any that keep to these rules, and one draw needn't show every extreme that they name: `block_rows`: the 11 entries of one column are distinct feature blocks. `section_count`: on one index of mp every column has all 11 sections live.
All inputs are finite; a program needn't handle non-finite values.
Results may differ from a plain program's by a relative error of at most 0.02.
Values may be sent and summed in bfloat16 or wider, within the bound.
A program may use at most 320 MiB of HBM per device.

v0:
```python
import jax
import jax.numpy as jnp
from jax import lax
from jax.sharding import PartitionSpec as P

gelu_coef = 0.044715
gelu_scale = 0.7978845608028654


def gelu_parts(preact):
    inside = gelu_scale * (preact + gelu_coef * preact * preact * preact)
    tanh_part = jnp.tanh(inside)
    activated = 0.5 * preact * (1.0 + tanh_part)
    derivative = 0.5 * (1.0 + tanh_part) + 0.5 * preact * (
        1.0 - tanh_part * tanh_part
    ) * gelu_scale * (1.0 + 3.0 * gelu_coef * preact * preact)
    return (activated, derivative)


def latent_total(partial_value):
    return lax.psum(partial_value.astype(jnp.bfloat16), "mp").astype(jnp.float32)


def feature_total(partial_value):
    return lax.psum_scatter(
        partial_value.astype(jnp.bfloat16), "mp", scatter_dimension=1, tiled=True
    ).astype(jnp.float32)


def shards(
    activations, out_grad, up_blocks, down_blocks, latent_in, latent_out, block_rows, section_count
):
    tok_rows = activations.shape[0]
    block_size = up_blocks.shape[0]
    slot_count = up_blocks.shape[1]
    columns = section_count.shape[0]
    sections_all = block_rows.shape[0]
    hidden_width = columns * block_size
    whole_in, whole_grad = (
        lax.all_gather(activations, "mp", axis=1, tiled=True),
        lax.all_gather(out_grad, "mp", axis=1, tiled=True),
    )
    feat_width = whole_in.shape[1]
    row_blocks = feat_width // block_size
    in_blocks = whole_in.reshape(tok_rows, row_blocks, block_size)
    grad_blocks = whole_grad.reshape(tok_rows, row_blocks, block_size)
    contract_last = (((1,), (1,)), ((), ()))
    contract_first = (((0,), (0,)), ((), ()))
    latent_part = lax.dot_general(
        activations, latent_in, contract_last, preferred_element_type=jnp.float32
    )
    latent = latent_total(latent_part).astype(jnp.bfloat16)

    def live_at(section_at):
        return (section_at < section_count).astype(jnp.float32)[None, :, None]

    def section_slab(blocks, section_at):
        return lax.dynamic_slice_in_dim(blocks, section_at * columns, columns, 1)

    def row_index_at(section_at):
        return lax.dynamic_index_in_dim(block_rows, section_at, 0, keepdims=False)

    def up_step(section_at, running):
        picked = jnp.take(in_blocks, row_index_at(section_at), axis=1)
        product = jnp.einsum(
            "rck,kcn->rcn",
            picked,
            section_slab(up_blocks, section_at),
            preferred_element_type=jnp.float32,
        )
        return running + product * live_at(section_at)

    sparse_pre = lax.fori_loop(
        0, sections_all, up_step, jnp.zeros((tok_rows, columns, block_size), jnp.float32)
    )
    preact = sparse_pre.reshape(tok_rows, hidden_width) + jnp.dot(
        latent, latent_out, preferred_element_type=jnp.float32
    )
    activated, derivative = gelu_parts(preact)
    hidden = activated.astype(jnp.bfloat16)
    hidden_blocks = hidden.reshape(tok_rows, columns, block_size)

    def down_step(section_at, running):
        out_total, back_total, down_total = running
        live_now = live_at(section_at)
        weights = section_slab(down_blocks, section_at)
        row_index = row_index_at(section_at)
        grad_piece = jnp.take(grad_blocks, row_index, axis=1)
        forward_piece = (
            jnp.einsum("rck,kcn->rcn", hidden_blocks, weights, preferred_element_type=jnp.float32)
            * live_now
        )
        out_total = out_total.at[:, row_index, :].add(forward_piece)
        back_total = (
            back_total
            + jnp.einsum("rcn,kcn->rck", grad_piece, weights, preferred_element_type=jnp.float32)
            * live_now
        )
        weight_grad = (
            jnp.einsum(
                "rck,rcn->kcn", hidden_blocks, grad_piece, preferred_element_type=jnp.float32
            )
            * live_now[0]
        )
        down_total = lax.dynamic_update_slice_in_dim(
            down_total, weight_grad, section_at * columns, 1
        )
        return (out_total, back_total, down_total)

    down_start = (
        jnp.zeros((tok_rows, row_blocks, block_size), jnp.float32),
        jnp.zeros((tok_rows, columns, block_size), jnp.float32),
        jnp.zeros((block_size, slot_count, block_size), jnp.float32),
    )
    out_part, hidden_grad, down_part = lax.fori_loop(0, sections_all, down_step, down_start)
    mixed = feature_total(out_part.reshape(tok_rows, feat_width)).astype(jnp.bfloat16)
    pre_grad = (hidden_grad.reshape(tok_rows, hidden_width) * derivative).astype(jnp.bfloat16)
    pre_blocks = pre_grad.reshape(tok_rows, columns, block_size)
    back_part = lax.dot_general(
        pre_grad, latent_out, contract_last, preferred_element_type=jnp.float32
    )
    back_latent = latent_total(back_part).astype(jnp.bfloat16)

    def in_step(section_at, running):
        in_total, up_total = running
        live_now = live_at(section_at)
        weights = section_slab(up_blocks, section_at)
        row_index = row_index_at(section_at)
        back_piece = (
            jnp.einsum("rcn,kcn->rck", pre_blocks, weights, preferred_element_type=jnp.float32)
            * live_now
        )
        in_total = in_total.at[:, row_index, :].add(back_piece)
        picked = jnp.take(in_blocks, row_index, axis=1)
        weight_grad = (
            jnp.einsum("rck,rcn->kcn", picked, pre_blocks, preferred_element_type=jnp.float32)
            * live_now[0]
        )
        up_total = lax.dynamic_update_slice_in_dim(up_total, weight_grad, section_at * columns, 1)
        return (in_total, up_total)

    in_start = (
        jnp.zeros((tok_rows, row_blocks, block_size), jnp.float32),
        jnp.zeros((block_size, slot_count, block_size), jnp.float32),
    )
    in_part, up_part = lax.fori_loop(0, sections_all, in_step, in_start)
    input_sum = feature_total(in_part.reshape(tok_rows, feat_width))
    input_grad = (
        input_sum + jnp.dot(back_latent, latent_in, preferred_element_type=jnp.float32)
    ).astype(jnp.bfloat16)
    latent_out_part = lax.dot_general(
        latent, pre_grad, contract_first, preferred_element_type=jnp.float32
    )
    latent_in_part = lax.dot_general(
        back_latent, activations, contract_first, preferred_element_type=jnp.float32
    )
    up_share, down_share, lin_share, lout_share = (
        lax.psum_scatter(
            up_part.astype(jnp.bfloat16), "dp", scatter_dimension=0, tiled=True
        ).astype(jnp.float32),
        lax.psum_scatter(
            down_part.astype(jnp.bfloat16), "dp", scatter_dimension=0, tiled=True
        ).astype(jnp.float32),
        lax.psum_scatter(
            latent_in_part.astype(jnp.bfloat16), "dp", scatter_dimension=0, tiled=True
        ).astype(jnp.float32),
        lax.psum_scatter(
            latent_out_part.astype(jnp.bfloat16), "dp", scatter_dimension=0, tiled=True
        ).astype(jnp.float32),
    )
    return (
        mixed,
        input_grad,
        up_share.astype(jnp.bfloat16),
        down_share.astype(jnp.bfloat16),
        lin_share.astype(jnp.bfloat16),
        lout_share.astype(jnp.bfloat16),
    )


def solution(mesh):
    return jax.shard_map(
        shards,
        mesh=mesh,
        in_specs=(
            P("dp", "mp"),
            P("dp", "mp"),
            P(None, "mp", None),
            P(None, "mp", None),
            P(None, "mp"),
            P(None, "mp"),
            P(None, "mp"),
            P("mp"),
        ),
        out_specs=(
            P("dp", "mp"),
            P("dp", "mp"),
            P("dp", "mp", None),
            P("dp", "mp", None),
            P("dp", "mp"),
            P("dp", "mp"),
        ),
        check_vma=False,
    )
```

profile of v0, /device:TPU:0, one launch (start us, length us, event | category | flops | bytes accessed | tf_op | source)
XLA Modules:
  0.0 2188.8 jit_solution(14491981513515651858)
XLA Ops:
  14.6 44.0 %all-gather.3.cloned.1.call-done = bf16[256,12288]{0,1:T(8,128)(2,1)} async-done(((bf16[256,1536]{0,1:T(8,128)(2,1)}), bf16[256,12288]{0,1:T(8,128)(2,1)}) %all-gather.3.cloned.1.call-update) | async-done | bytes 6291472 | tf_op jit(solution)/shard_map/all_gather | solution.py:40
  67.2 171.4 %while.48 = (s32[]{:T(128)}, f32[256,48,128]{0,2,1:T(8,128)}, bf16[128,528,128]{2,1,0:T(8,128)(2,1)}, s32[11,48]{1,0:T(8,128)}, bf16[256,96,128]{2,0,1:T(8,128)(...) while((s32[]{:T(128)}, f32[256,48,128]{0,2,1:T(8,128)}, ...), condition=%wide.region_1.3_spmd.clone, body=%wide.region_0.2_spmd.clone.sunk | while | flops 408946048 | bytes 26745416 | solution.py:73
  275.7 620.1 %while.49 = (s32[]{:T(128)}, f32[256,96,128]{2,0,1:T(8,128)}, f32[256,48,128]{0,2,1:T(8,128)}, bf16[128,528,128]{2,1,0:T(8,128)(2,1)}, s32[11,48]{1,0:T(8,128)},...) while((s32[]{:T(128)}, f32[256,96,128]{2,0,1:T(8,128)}, ...), condition=%wide.region_5.7_spmd.clone, body=%wide.region_3.6_spmd.clone.sunk | while | flops 1220544000 | bytes 111681168 | solution.py:115
  295.2 14.9 scatter_fusion.1
  349.9 14.9 scatter_fusion.1
  406.4 14.8 scatter_fusion.1
  462.9 14.9 scatter_fusion.1
  519.4 14.9 scatter_fusion.1
  576.0 14.8 scatter_fusion.1
  632.5 14.9 scatter_fusion.1
  689.0 14.9 scatter_fusion.1
  745.5 15.0 scatter_fusion.1
  802.2 14.8 scatter_fusion.1
  858.7 14.9 scatter_fusion.1
  929.5 443.4 %while.47 = (s32[]{:T(128)}, f32[256,96,128]{2,0,1:T(8,128)}, bf16[128,528,128]{2,1,0:T(8,128)(2,1)}, s32[11,48]{1,0:T(8,128)}, bf16[128,528,128]{2,1,0:T(8,128)...) while((s32[]{:T(128)}, f32[256,96,128]{2,0,1:T(8,128)}, ...), condition=%wide.region_9.11_spmd, body=%wide.region_7.10_spmd.sunk | while | flops 811599360 | bytes 75503992 | solution.py:146
  954.9 14.9 scatter_fusion
  995.2 14.9 scatter_fusion
  1035.5 15.0 scatter_fusion
  1075.9 14.8 scatter_fusion
  1116.1 14.9 scatter_fusion
  1156.5 14.9 scatter_fusion
  1196.7 14.9 scatter_fusion
  1237.0 14.9 scatter_fusion
  1277.4 14.8 scatter_fusion
  1317.6 15.0 scatter_fusion
  1358.0 14.9 scatter_fusion
  1399.6 44.0 %reduce-scatter.9.cloned.1.call-done = bf16[256,1536]{1,0:T(8,128)(2,1)} async-done(((bf16[256,12288]{1,0:T(8,128)(2,1)}), bf16[256,1536]{1,0:T(8,128)(2,1)}) %reduce-scatter.9.cloned.1.call-update) | async-done | bytes 786448 | tf_op jit(solution)/shard_map/reduce_scatter | solution.py:25
  1446.2 23.3 %reduce-scatter.15.cloned.1.call-done = bf16[64,1536]{1,0:T(8,128)(2,1)} async-done(((bf16[256,1536]{1,0:T(8,128)(2,1)}), bf16[64,1536]{1,0:T(8,128)(2,1)}) %reduce-scatter.15.cloned.1.call-update) | async-done | bytes 196624 | tf_op jit(solution)/shard_map/reduce_scatter | solution.py:164
  1469.5 62.8 %reduce-scatter.17.cloned.1.call-done = bf16[64,6144]{1,0:T(8,128)(2,1)} async-done(((bf16[256,6144]{1,0:T(8,128)(2,1)}), bf16[64,6144]{1,0:T(8,128)(2,1)}) %reduce-scatter.17.cloned.1.call-update) | async-done | bytes 786448 | tf_op jit(solution)/shard_map/reduce_scatter | solution.py:167
  1532.3 65.6 %reduce-scatter.7.cloned.1.call-done = bf16[256,1536]{1,0:T(8,128)(2,1)} async-done(((bf16[256,12288]{1,0:T(8,128)(2,1)}), bf16[256,1536]{1,0:T(8,128)(2,1)}) %reduce-scatter.7.cloned.1.call-update) | async-done | bytes 786448 | tf_op jit(solution)/shard_map/reduce_scatter | solution.py:25
  1597.8 291.8 %reduce-scatter.11.cloned.1.call-done = bf16[32,528,128]{2,1,0:T(8,128)(2,1)} async-done(((bf16[128,528,128]{2,1,0:T(8,128)(2,1)}), bf16[32,528,128]{2,1,0:T(8,128)(2,1)}) %reduce-scatter.11.cloned.1.call-update) | async-done | bytes 4325392 | tf_op jit(solution)/shard_map/reduce_scatter | solution.py:158
  1889.6 292.3 %reduce-scatter.13.cloned.1.call-done = bf16[32,528,128]{2,1,0:T(8,128)(2,1)} async-done(((bf16[128,528,128]{2,1,0:T(8,128)(2,1)}), bf16[32,528,128]{2,1,0:T(8,128)(2,1)}) %reduce-scatter.13.cloned.1.call-update) | async-done | bytes 4325392 | tf_op jit(solution)/shard_map/reduce_scatter | solution.py:161
  (410 shorter events, 1022.8 us)
Async XLA Ops:
  7.2 237.9 %copy-start = (bf16[256,6144]{1,0:T(8,128)(2,1)S(1)}, bf16[256,6144]{1,0:T(8,128)(2,1)}, u32[]{:S(2)}) copy-start(bf16[256,6144]{1,0:T(8,128)(2,1)} %param.21) | copy-start | bytes 9437188
  7.2 51.4 %all-gather.3.cloned.1.call-start = ((), (), s32[]{:S(2)}) async-start(), calls=%async_computation.6 | async-start | bytes 7077888 | tf_op jit(solution)/shard_map/all_gather | solution.py:40
  9.7 235.4 %all-reduce.3.cloned.1.call-start = ((), (), s32[]{:S(2)}) async-start(), calls=%async_computation.7 | async-start | bytes 262144 | tf_op jit(solution)/shard_map/psum | solution.py:21
  12.2 242.6 %all-gather.5.cloned.1.call-start = ((), (), s32[]{:S(2)}) async-start(), calls=%async_computation.8 | async-start | bytes 7077888 | tf_op jit(solution)/shard_map/all_gather | solution.py:41
  14.6 1366.6 %all-reduce.5.cloned.1.call-start = ((), (), s32[]{:S(2)}) async-start(), calls=%async_computation.11 | async-start | bytes 262144 | tf_op jit(solution)/shard_map/psum | solution.py:21
  58.6 8.6 copy-start.8
  370.3 8.5 copy-start.1
  370.3 8.5 copy-start.2
  426.8 8.5 copy-start.1
  426.8 8.5 copy-start.2
  483.3 8.5 copy-start.1
  483.3 8.5 copy-start.2
  539.9 8.5 copy-start.1
  539.9 8.5 copy-start.2
  596.3 8.5 copy-start.1
  596.3 8.5 copy-start.2
  652.9 8.5 copy-start.1
  652.9 8.5 copy-start.2
  709.4 8.5 copy-start.1
  709.4 8.5 copy-start.2
  766.0 8.5 copy-start.1
  766.0 8.5 copy-start.2
  822.5 8.5 copy-start.2
  879.1 8.5 copy-start.1
  879.1 8.5 copy-start.2
  917.1 526.5 %reduce-scatter.9.cloned.1.call-start = ((), (), s32[]{:S(2)}) async-start(), calls=%async_computation.10 | async-start | bytes 7077888 | tf_op jit(solution)/shard_map/reduce_scatter | solution.py:25
  1381.0 88.4 %reduce-scatter.15.cloned.1.call-start = ((), (), s32[]{:S(2)}) async-start(), calls=%async_computation.14 | async-start | bytes 983040 | tf_op jit(solution)/shard_map/reduce_scatter | solution.py:164
  1383.6 148.7 %reduce-scatter.17.cloned.1.call-start = ((), (), s32[]{:S(2)}) async-start(), calls=%async_computation.15 | async-start | bytes 3932160 | tf_op jit(solution)/shard_map/reduce_scatter | solution.py:167
  1388.3 209.6 %reduce-scatter.7.cloned.1.call-start = ((), (), s32[]{:S(2)}) async-start(), calls=%async_computation.9 | async-start | bytes 7077888 | tf_op jit(solution)/shard_map/reduce_scatter | solution.py:25
  1398.3 491.4 %reduce-scatter.11.cloned.1.call-start = ((), (), s32[]{:S(2)}) async-start(), calls=%async_computation.12 | async-start | bytes 21626880 | tf_op jit(solution)/shard_map/reduce_scatter | solution.py:158
  1399.0 783.0 %reduce-scatter.13.cloned.1.call-start = ((), (), s32[]{:S(2)}) async-start(), calls=%async_computation.13 | async-start | bytes 21626880 | tf_op jit(solution)/shard_map/reduce_scatter | solution.py:161
  1399.0 44.5 %copy-start.7 = (bf16[256,256]{1,0:T(8,128)(2,1)S(1)}, bf16[256,256]{1,0:T(8,128)(2,1)}, u32[]{:S(2)}) copy-start(bf16[256,256]{1,0:T(8,128)(2,1)} %all-reduce.5.cloned.1.call-done) | copy-start | bytes 393220
  (17 other events, 119.9 us)
Sparse Core Ops, SparseCore 0:
  10.4 48.1 all-gather.2
  62.2 53.4 all-reduce.2
  118.2 44.7 all-gather.4
  917.2 53.8 all-reduce.4
  1381.2 62.3 reduce-scatter.8
  1446.3 23.1 reduce-scatter.14
  1472.3 59.9 reduce-scatter.16
  1536.2 61.5 reduce-scatter.6
  1600.8 288.7 reduce-scatter.10
  1892.4 289.4 reduce-scatter.12
where the time goes:
time: 2200 us; the launch traced here: 2190 us
  waiting for transfers between devices  825 us (38%)
  local copies, waits for them, and re-layouts  579 us (26%)
  other arithmetic  394 us (18%)
  matrix products  375 us (17%)
    reduce_scatter x1, waiting for transfers between devices, shards(): lax.psum_scatter(down_part.astype(jnp.bfloat16), 'dp', scatter_dimension=...  292 us
    reduce_scatter x1, waiting for transfers between devices, shards(): lax.psum_scatter(up_part.astype(jnp.bfloat16), 'dp', scatter_dimension=0,...  292 us
    scatter-add x11, other arithmetic, in_step(): in_total = in_total.at[:, row_index, :].add(back_piece)  164 us
    scatter-add x11, other arithmetic, down_step(): out_total = out_total.at[:, row_index, :].add(forward_piece)  164 us
    reduce_scatter x2, waiting for transfers between devices, feature_total(): lax.psum_scatter(partial_value.astype(jnp.bfloat16), 'mp', scatter_dimens...  110 us
    dot_general x11, matrix products, down_step(): jnp.einsum('rcn,kcn->rck', grad_piece, weights, preferred_element_type=jn...  91.6 us
    dot_general x11, matrix products, up_step(): jnp.einsum('rck,kcn->rcn', picked, section_slab(up_blocks, section_at), p...  86.1 us
    dynamic_slice x33, local copies, waits for them, and re-layouts, section_slab(): return lax.dynamic_slice_in_dim(blocks, section_at * columns, columns, 1)  77.2 us
  transfers between devices with their start and end apart: 10, of which 7 were waited for; matrix products, arithmetic and copies ran while one was open for 31% of the time, Pallas kernels for 0%

commit v1 on v0

v1 whole, which is shorter than its diff:
```python
import functools

import jax
import jax.numpy as jnp
from jax import lax
from jax.experimental import pallas as pl
from jax.experimental.pallas import tpu as pltpu
from jax.sharding import PartitionSpec as P

gelu_coef = 0.044715
gelu_scale = 0.7978845608028654
vmem_limit = 60 * 1024 * 1024
bf16 = jnp.bfloat16
f32 = jnp.float32
last_last = (((1,), (1,)), ((), ()))
first_first = (((0,), (0,)), ((), ()))


def gelu_parts(preact):
    inside = gelu_scale * (preact + gelu_coef * preact * preact * preact)
    tanh_part = jnp.tanh(inside)
    activated = 0.5 * preact * (1.0 + tanh_part)
    derivative = 0.5 * (1.0 + tanh_part) + 0.5 * preact * (
        1.0 - tanh_part * tanh_part
    ) * gelu_scale * (1.0 + 3.0 * gelu_coef * preact * preact)
    return (activated, derivative)


def picked_blocks(rows_ref, source_ref, column, sections, axis):
    return jnp.concatenate(
        [source_ref[rows_ref[section_at, column]] for section_at in range(sections)], axis=axis
    )


def forward_kernel(
    sections, rows_ref, in_ref, grad_ref, up_ref, down_ref, latent_ref, lout_ref, hid_ref, pre_ref
):
    column = pl.program_id(0)
    in_wide = picked_blocks(rows_ref, in_ref, column, sections, 1)
    preact = jnp.dot(in_wide, up_ref[0], preferred_element_type=f32) + jnp.dot(
        latent_ref[...], lout_ref[...], preferred_element_type=f32
    )
    activated, derivative = gelu_parts(preact)
    hid_ref[...] = activated.astype(bf16)
    grad_wide = picked_blocks(rows_ref, grad_ref, column, sections, 1)
    hidden_grad = lax.dot_general(grad_wide, down_ref[0], last_last, preferred_element_type=f32)
    pre_ref[...] = (hidden_grad * derivative).astype(bf16)


def spread_kernel(
    sections,
    width,
    rows_ref,
    grad_ref,
    up_ref,
    down_ref,
    hid_ref,
    pre_ref,
    lout_ref,
    mask_ref,
    mixed_ref,
    back_ref,
    dgrad_ref,
    lat_ref,
    out_total,
    in_total,
    lat_total,
):
    column = pl.program_id(0)
    row_blocks = out_total.shape[0]

    @pl.when(column == 0)
    def _():
        @pl.loop(0, row_blocks)
        def _(block_at):
            out_total[block_at] = jnp.zeros(out_total.shape[1:], f32)
            in_total[block_at] = jnp.zeros(in_total.shape[1:], f32)

        lat_total[...] = jnp.zeros_like(lat_total)

    hidden = hid_ref[...]
    pre = pre_ref[...]
    grad_wide = picked_blocks(rows_ref, grad_ref, column, sections, 1)
    weight_grad = lax.dot_general(hidden, grad_wide, first_first, preferred_element_type=f32)
    weight_grad = (weight_grad * mask_ref[0]).astype(bf16)
    dgrad_ref[...] = weight_grad.reshape(dgrad_ref.shape)
    forward = jnp.dot(hidden, down_ref[0], preferred_element_type=f32)
    backward = lax.dot_general(pre, up_ref[0], last_last, preferred_element_type=f32)
    for section_at in range(sections):
        row = rows_ref[section_at, column]
        cut = slice(section_at * width, (section_at + 1) * width)
        out_total[row] += forward[:, cut]
        in_total[row] += backward[:, cut]
    lat_total[...] += lax.dot_general(pre, lout_ref[...], last_last, preferred_element_type=f32)

    @pl.when(column == pl.num_programs(0) - 1)
    def _():
        @pl.loop(0, row_blocks)
        def _(block_at):
            mixed_ref[block_at] = out_total[block_at].astype(bf16)
            back_ref[block_at] = in_total[block_at].astype(bf16)

        lat_ref[...] = lat_total[...].astype(bf16)


def up_grad_kernel(
    sections, rows_ref, count_ref, part_ref, latent_ref, pre_ref, ugrad_ref, lgrad_ref
):
    column = pl.program_id(0)
    pre = pre_ref[...].reshape(-1, pre_ref.shape[-1])
    part_rows = part_ref.shape[1]
    stacked = picked_blocks(rows_ref, part_ref, column, sections, 0)
    product = jnp.dot(stacked, pre, preferred_element_type=f32)
    for section_at in range(sections):
        live = (section_at < count_ref[column]).astype(f32)
        ugrad_ref[0, section_at] = (
            product[section_at * part_rows : (section_at + 1) * part_rows] * live
        ).astype(bf16)
    lgrad_ref[...] = jnp.dot(latent_ref[...], pre, preferred_element_type=f32).astype(bf16)


def whole_spec():
    return pl.BlockSpec(memory_space=pltpu.VMEM)


def latent_total(partial_value):
    parts = lax.all_gather(partial_value.astype(bf16), "mp", axis=0)
    return jnp.sum(parts.astype(f32), axis=0).astype(bf16)


def shards(
    activations, out_grad, up_blocks, down_blocks, latent_in, latent_out, block_rows, section_count
):
    n_dp = lax.axis_size("dp")
    tok_rows, feat_local = activations.shape
    width = up_blocks.shape[0]
    columns = section_count.shape[0]
    sections = block_rows.shape[0]
    own_blocks = feat_local // width
    rank = latent_in.shape[0]
    hidden_width = columns * width
    span = sections * width
    cut_rows = width // n_dp
    rank_rows = rank // n_dp

    def by_block(values):
        return jnp.transpose(values.reshape(tok_rows, own_blocks, width), (1, 0, 2))

    def from_blocks(values):
        return jnp.transpose(values, (1, 0, 2)).reshape(tok_rows, feat_local)

    in_blocks = lax.all_gather(by_block(activations), "mp", axis=0, tiled=True)
    latent = latent_total(
        lax.dot_general(activations, latent_in, last_last, preferred_element_type=f32)
    )
    grad_blocks = lax.all_gather(by_block(out_grad), "mp", axis=0, tiled=True)
    sliced = jnp.transpose(
        activations.reshape(tok_rows, own_blocks, n_dp, cut_rows), (2, 1, 3, 0)
    )
    exchanged = lax.all_to_all(sliced, "dp", split_axis=0, concat_axis=0, tiled=True)
    exchanged = jnp.transpose(exchanged, (1, 2, 0, 3)).reshape(
        own_blocks, cut_rows, n_dp * tok_rows
    )
    exchanged, grad_blocks = lax.optimization_barrier((exchanged, grad_blocks))
    in_cuts = lax.all_gather(exchanged, "mp", axis=0, tiled=True)
    row_blocks = in_blocks.shape[0]

    live = jnp.arange(sections)[:, None] < section_count[None, :]
    live_slots = live.reshape(1, sections * columns, 1)
    zero = jnp.zeros((), bf16)
    up_live = jnp.where(live_slots, up_blocks, zero).reshape(width, sections, columns, width)
    down_live = jnp.where(live_slots, down_blocks, zero).reshape(width, sections, columns, width)
    up_cols = jnp.transpose(up_live, (2, 1, 0, 3)).reshape(columns, span, width)
    down_cols = jnp.transpose(down_live, (2, 0, 1, 3)).reshape(columns, width, span)
    mask = jnp.repeat(live.T.astype(f32), width, axis=1).reshape(columns, 1, span)

    def column_block(height):
        return pl.BlockSpec((height, width), lambda column, *_: (0, column))

    up_spec = pl.BlockSpec((1, span, width), lambda column, *_: (column, 0, 0))
    down_spec = pl.BlockSpec((1, width, span), lambda column, *_: (column, 0, 0))
    params = pltpu.CompilerParams(
        dimension_semantics=("arbitrary",), vmem_limit_bytes=vmem_limit
    )
    slab = jax.ShapeDtypeStruct((tok_rows, hidden_width), bf16)
    pair_flops = 2 * tok_rows * hidden_width * span
    weight_bytes = 2 * width * width * sections * columns

    hidden, pre_grad = pl.pallas_call(
        functools.partial(forward_kernel, sections),
        grid_spec=pltpu.PrefetchScalarGridSpec(
            num_scalar_prefetch=1,
            grid=(columns,),
            in_specs=[
                whole_spec(),
                whole_spec(),
                up_spec,
                down_spec,
                whole_spec(),
                column_block(rank),
            ],
            out_specs=[column_block(tok_rows), column_block(tok_rows)],
        ),
        out_shape=[slab, slab],
        compiler_params=params,
        cost_estimate=pl.CostEstimate(
            flops=2 * pair_flops, bytes_accessed=3 * weight_bytes, transcendentals=0
        ),
        name="forward",
    )(block_rows, in_blocks, grad_blocks, up_cols, down_cols, latent, latent_out)

    in_cuts, pre_sent = lax.optimization_barrier((in_cuts, pre_grad))
    pre_all = lax.all_gather(pre_sent, "dp", axis=0)

    totals = jax.ShapeDtypeStruct((row_blocks, tok_rows, width), bf16)
    mixed_part, in_part, down_part, back_part = pl.pallas_call(
        functools.partial(spread_kernel, sections, width),
        grid_spec=pltpu.PrefetchScalarGridSpec(
            num_scalar_prefetch=1,
            grid=(columns,),
            in_specs=[
                whole_spec(),
                up_spec,
                down_spec,
                column_block(tok_rows),
                column_block(tok_rows),
                column_block(rank),
                pl.BlockSpec((1, 1, span), lambda column, *_: (column, 0, 0)),
            ],
            out_specs=[
                whole_spec(),
                whole_spec(),
                pl.BlockSpec((n_dp, 1, cut_rows, span), lambda column, *_: (0, column, 0, 0)),
                whole_spec(),
            ],
            scratch_shapes=[
                pltpu.VMEM((row_blocks, tok_rows, width), f32),
                pltpu.VMEM((row_blocks, tok_rows, width), f32),
                pltpu.VMEM((tok_rows, rank), f32),
            ],
        ),
        out_shape=[
            totals,
            totals,
            jax.ShapeDtypeStruct((n_dp, columns, cut_rows, span), bf16),
            jax.ShapeDtypeStruct((tok_rows, rank), bf16),
        ],
        compiler_params=params,
        cost_estimate=pl.CostEstimate(
            flops=3 * pair_flops, bytes_accessed=4 * weight_bytes, transcendentals=0
        ),
        name="spread",
    )(block_rows, grad_blocks, up_cols, down_cols, hidden, pre_grad, latent_out, mask)

    pre_all, mixed_part, in_part, down_part, back_part = lax.optimization_barrier(
        (pre_all, mixed_part, in_part, down_part, back_part)
    )
    back_latent = latent_total(back_part)
    down_share = lax.psum_scatter(down_part, "dp", scatter_dimension=0, tiled=True)
    down_share, mixed_part, in_part = lax.optimization_barrier((down_share, mixed_part, in_part))
    mixed = from_blocks(lax.psum_scatter(mixed_part, "mp", scatter_dimension=0, tiled=True))
    input_sum = from_blocks(
        lax.psum_scatter(in_part, "mp", scatter_dimension=0, tiled=True).astype(f32)
    )
    input_grad = (
        input_sum + jnp.dot(back_latent, latent_in, preferred_element_type=f32)
    ).astype(bf16)
    down_share = jnp.transpose(
        down_share.reshape(columns, cut_rows, sections, width), (1, 2, 0, 3)
    ).reshape(cut_rows, sections * columns, width)

    latent_all = lax.all_gather(latent, "dp", axis=0)
    latent_cut = lax.dynamic_slice_in_dim(
        latent_all, lax.axis_index("dp") * rank_rows, rank_rows, 2
    )
    latent_cut = jnp.transpose(latent_cut, (2, 0, 1)).reshape(rank_rows, n_dp * tok_rows)

    up_part, lout_share = pl.pallas_call(
        functools.partial(up_grad_kernel, sections),
        grid_spec=pltpu.PrefetchScalarGridSpec(
            num_scalar_prefetch=2,
            grid=(columns,),
            in_specs=[
                whole_spec(),
                whole_spec(),
                pl.BlockSpec((n_dp, tok_rows, width), lambda column, *_: (0, 0, column)),
            ],
            out_specs=[
                pl.BlockSpec((1, sections, cut_rows, width), lambda column, *_: (column, 0, 0, 0)),
                column_block(rank_rows),
            ],
        ),
        out_shape=[
            jax.ShapeDtypeStruct((columns, sections, cut_rows, width), bf16),
            jax.ShapeDtypeStruct((rank_rows, hidden_width), bf16),
        ],
        compiler_params=params,
        cost_estimate=pl.CostEstimate(
            flops=pair_flops, bytes_accessed=weight_bytes, transcendentals=0
        ),
        name="up_grad",
    )(block_rows, section_count, in_cuts, latent_cut, pre_all)
    up_share = jnp.transpose(up_part, (2, 1, 0, 3)).reshape(cut_rows, sections * columns, width)

    latent_in_part = lax.dot_general(
        back_latent, activations, first_first, preferred_element_type=f32
    )
    lin_share = lax.psum_scatter(
        latent_in_part.astype(bf16), "dp", scatter_dimension=0, tiled=True
    )
    return (mixed, input_grad, up_share, down_share, lin_share, lout_share)


def solution(mesh):
    return jax.shard_map(
        shards,
        mesh=mesh,
        in_specs=(
            P("dp", "mp"),
            P("dp", "mp"),
            P(None, "mp", None),
            P(None, "mp", None),
            P(None, "mp"),
            P(None, "mp"),
            P(None, "mp"),
            P("mp"),
        ),
        out_specs=(
            P("dp", "mp"),
            P("dp", "mp"),
            P("dp", "mp", None),
            P("dp", "mp", None),
            P("dp", "mp"),
            P("dp", "mp"),
        ),
        check_vma=False,
    )
```

time: 2200 us -> 901 us (0.41)
  local copies, waits for them, and re-layouts: 579 us -> 102 us
  matrix products: 375 us -> 4.77 us
  other arithmetic: 394 us -> 28.5 us
  waiting for transfers between devices: 825 us -> 553 us
  Pallas kernels: 0 us -> 150 us
  blocking collectives: 0 us -> 42.4 us
    reduce_scatter x6 -> x4, waiting for transfers between devices: 780 us -> 352 us  [the longest x1 288 us: shards(): lax.psum_scatter(down_part, 'dp', scatter_dimension=0, tiled=True)]
    dot_general x72 -> x3, matrix products: 375 us -> 4.77 us  [the longest x1 2.19 us: shards(): lax.dot_general(activations, latent_in, last_last, preferred_element_type...]
    scatter-add x22 -> x0, other arithmetic: 328 us -> none  [the longest x11 164 us: in_step(): in_total = in_total.at[:, row_index, :].add(back_piece)]
    gather x33 -> x0, local copies, waits for them, and re-layouts: 182 us -> none  [the longest x11 60.6 us: up_step(): picked = jnp.take(in_blocks, row_index_at(section_at), axis=1)]
    all_gather x2 -> x6, waiting for transfers between devices: 44 us -> 199 us  [the longest x1 156 us: shards(): pre_all = lax.all_gather(pre_sent, 'dp', axis=0)]
    pallas_call x0 -> x3, Pallas kernels: none -> 150 us  [the longest x1 62.5 us: shards(): pl.pallas_call(functools.partial(spread_kernel, sections, width), grid_sp...]
    mul x22 -> x0, local copies, waits for them, and re-layouts: 146 us -> none  [the longest x11 72.9 us: down_step(): jnp.einsum('rck,kcn->rcn', hidden_blocks, weights, preferred_element_type...]
    dynamic_update_slice x33 -> x0, local copies, waits for them, and re-layouts: 106 us -> none  [the longest x22 62.5 us: down_step(): lax.dynamic_update_slice_in_dim(down_total, weight_grad, section_at * col...]
  transfers between devices with their start and end apart: 10 -> 10, of which waited for: 7 -> 6; matrix products, arithmetic and copies ran while one was open for 31% -> 15% of each run, Pallas kernels for 0% -> 17%
where the time goes in v1:
time: 901 us; the launch traced here: 895 us
  waiting for transfers between devices  553 us (61%)
  Pallas kernels  150 us (17%)
  local copies, waits for them, and re-layouts  102 us (11%)
  blocking collectives  42.4 us (5%)
  other arithmetic  28.5 us (3%)
  between operations  14.3 us (2%)
    reduce_scatter x1, waiting for transfers between devices, shards(): lax.psum_scatter(down_part, 'dp', scatter_dimension=0, tiled=True)  288 us
    all_gather x1, waiting for transfers between devices, shards(): pre_all = lax.all_gather(pre_sent, 'dp', axis=0)  156 us
    pallas_call x1, Pallas kernels, shards(): pl.pallas_call(functools.partial(spread_kernel, sections, width), grid_sp...  62.5 us
    pallas_call x1, Pallas kernels, shards(): pl.pallas_call(functools.partial(forward_kernel, sections), grid_spec=plt...  49.6 us
    reduce_scatter x1, waiting for transfers between devices, shards(): lax.psum_scatter(mixed_part, 'mp', scatter_dimension=0, tiled=True)  41.9 us
    pallas_call x1, Pallas kernels, shards(): pl.pallas_call(functools.partial(up_grad_kernel, sections), grid_spec=plt...  38.2 us
    all_to_all x1, blocking collectives, shards(): lax.all_to_all(sliced, 'dp', split_axis=0, concat_axis=0, tiled=True)  26.3 us
    all_gather x2, waiting for transfers between devices, latent_total(): parts = lax.all_gather(partial_value.astype(bf16), 'mp', axis=0)  25.8 us
  transfers between devices with their start and end apart: 10, of which 6 were waited for; matrix products, arithmetic and copies ran while one was open for 15% of the time, Pallas kernels for 17%

profile of v1, /device:TPU:0, one launch (start us, length us, event | category | flops | bytes accessed | tf_op | source)
XLA Modules:
  0.0 895.4 jit_solution(16342606379663630961)
XLA Ops:
  7.2 1.5 copy.74
  8.8 1.2 copy.75
  10.0 2.2 convolution_convert_fusion.1
  12.5 1.2 copy.77
  13.8 26.3 %all_to_all.5 = bf16[4,12,32,256]{3,2,1,0:T(8,128)(2,1)S(1)} all-to-all(bf16[4,12,32,256]{3,2,1,0:T(8,128)(2,1)S(1)} %copy.72), channel_id=1, replica_groups=mesh['dp'=4,'mp'=8] {'dp'}, dimensions={0} | all-to-all | bytes 1572864 | tf_op jit(solution)/shard_map/all_to_all | solution.py:160
  40.1 1.0 copy.91
  41.1 17.5 %all-gather.11.cloned.1.call-done.grad_ref = bf16[96,256,128]{2,1,0:T(8,128)(2,1)} async-done(((bf16[12,256,128]{2,1,0:T(8,128)(2,1)}), bf16[96,256,128]{2,1,0:T(8,128)(2,1)}) %all-gather.11.cloned.1.call-update) | async-done | bytes 6291472 | tf_op jit(solution)/shard_map/all_gather | solution.py:156
  58.8 23.7 %broadcast_select_fusion = (bf16[128,528,128]{2,1,0:T(8,128)(2,1)}, bf16[128,528,128]{2,1,0:T(8,128)(2,1)}) fusion(bf16[128,528,128]{2,1,0:T(8,128)(2,1)} %param.11, pred[528]{0:T(1024)(128)(4,1)S(1)} %lt.33, bf16[128,528,128]{2,1,0:T(8,128)(2,1)} %param.10), kind=kLoop, calls=%fused_computation | loop fusion | flops 17301504 | bytes 69206544 | tf_op jit(solution)/shard_map/jit(_where)/select_n | solution.py:172
  82.5 22.7 %copy.79 = bf16[48,128,11,128]{1,3,2,0:T(8,128)(2,1)} copy(bf16[48,128,11,128]{3,0,2,1:T(8,128)(2,1)} %bitcast.47) | data formatting | bytes 34603008 | tf_op jit(solution)/shard_map/transpose | solution.py:174
  105.3 21.5 %copy.80.down_ref = bf16[48,128,1408]{2,1,0:T(8,128)(2,1)} copy(bf16[48,128,1408]{1,2,0:T(8,128)(2,1)} %bitcast.48) | data formatting | bytes 34603008 | tf_op jit(solution)/shard_map/reshape | solution.py:174
  126.8 18.4 %copy.78 = bf16[128,11,48,128]{3,0,1,2:T(8,128)(2,1)} copy(bf16[128,11,48,128]{3,2,1,0:T(8,128)(2,1)} %bitcast.46) | data formatting | bytes 34603008 | tf_op jit(solution)/shard_map/reshape | solution.py:171
  145.1 2.1 reduce_sum.24.latent_ref
  147.2 49.6 %forward.1 = (bf16[256,6144]{1,0:T(8,128)(2,1)}, bf16[256,6144]{1,0:T(8,128)(2,1)}) custom-call(s32[11,48]{1,0:T(8,128)} %rows_ref.5, bf16[96,256,128]{2,1,0:T(8,128)(2,1)} %all-gather.15.cloned.1.call-done.in_ref, bf16[96,256,128]{2,1,0:T(8,128)(2,1)} %all-gather.11.cloned.1.call-done.grad_ref, bf16[48,1408,128]{2,1,0:T(8,128)(2,1)} %bitcast.44, ...), custom_call_target="tpu_custom_call" | custom-call | flops 8858370048 | bytes 51904512 | tf_op jit(solution)/shard_map/forward/pallas_call | solution.py:189
  198.1 62.5 %spread.1 = (bf16[96,256,128]{2,1,0:T(8,128)(2,1)}, bf16[96,256,128]{2,1,0:T(8,128)(2,1)}, bf16[4,48,32,1408]{3,2,1,0:T(8,128)(2,1)}, bf16[256,256]{1,0:T(8,128)(2,1)}) custom-call(s32[11,48]{1,0:T(8,128)} %rows_ref.5, bf16[96,256,128]{2,1,0:T(8,128)(2,1)} %all-gather.11.cloned.1.call-done.grad_ref, bf16[48,1408,128]{2,1,0:T(8,128)(2,1)} %bitcast.45, ...), custom_call_target="tpu_custom_call" | custom-call | flops 13287555072 | bytes 69206016 | tf_op jit(solution)/shard_map/spread/pallas_call | solution.py:216
  260.7 155.8 %all-gather.19.cloned.1.call-done = bf16[1024,6144]{1,0:T(8,128)(2,1)} async-done(((bf16[256,6144]{1,0:T(8,128)(2,1)}), bf16[1024,6144]{1,0:T(8,128)(2,1)}) %all-gather.19.cloned.1.call-update) | async-done | bytes 12582928 | tf_op jit(solution)/shard_map/all_gather | solution.py:213
  417.3 288.4 %reduce-scatter.5.cloned.1.call-done = bf16[1,48,32,1408]{3,2,1,0:T(8,128)(2,1)} async-done(((bf16[4,48,32,1408]{3,2,1,0:T(8,128)(2,1)}), bf16[1,48,32,1408]{3,2,1,0:T(8,128)(2,1)}) %reduce-scatter.5.cloned.1.call-update) | async-done | bytes 4325392 | tf_op jit(solution)/shard_map/reduce_scatter | solution.py:259
  706.5 25.8 %all-gather.21.cloned.1.call-done = bf16[2048,256]{1,0:T(8,128)(2,1)} async-done(((bf16[256,256]{1,0:T(8,128)(2,1)}), bf16[2048,256]{1,0:T(8,128)(2,1)}) %all-gather.21.cloned.1.call-update) | async-done | bytes 1048592 | tf_op jit(solution)/shard_map/all_gather | solution.py:127
  732.3 1.4 reduce_sum.25
  733.7 1.3 convolution_convert_fusion
  735.0 16.2 %all-gather.3 = bf16[1024,256]{1,0:T(8,128)(2,1)S(1)} all-gather(bf16[256,256]{1,0:T(8,128)(2,1)S(1)} %copy-done.2), channel_id=5, replica_groups=mesh['dp'=4,'mp'=8] {'dp'}, dimensions={0}, use_global_device_ids=true | all-gather | bytes 655360 | tf_op jit(solution)/shard_map/all_gather | solution.py:272
  752.2 38.2 %up_grad.1 = (bf16[48,11,32,128]{3,2,1,0:T(8,128)(2,1)}, bf16[64,6144]{1,0:T(8,128)(2,1)}) custom-call(s32[11,48]{1,0:T(8,128)} %rows_ref.5, s32[48]{0:T(128)} %count_ref.1, bf16[96,32,1024]{2,1,0:T(8,128)(2,1)} %all-gather.13.cloned.1.call-done.part_ref, bf16[64,1024]{1,0:T(8,128)(2,1)} %bitcast.65, bf16[4,256,6144]{2,1,0:T(8,128)(2,1)} %bitcast.50), custom_call_target="tpu_custom_call" | custom-call | flops 4429185024 | bytes 17301504 | tf_op jit(solution)/shard_map/up_grad/pallas_call | solution.py:278
  790.4 6.0 copy.87
  796.4 9.2 %reshape.86 = bf16[48,32,11,128]{3,2,1,0:T(8,128)(2,1)} reshape(bf16[1,48,32,1408]{3,2,1,0:T(8,128)(2,1)} %reduce-scatter.5.cloned.1.call-done) | data formatting | bytes 8650752 | tf_op jit(solution)/shard_map/reshape | solution.py:269
  805.6 10.3 %copy.88 = bf16[32,11,48,128]{3,2,1,0:T(8,128)(2,1)} copy(bf16[32,11,48,128]{3,1,0,2:T(8,128)(2,1)} %bitcast.49) | data formatting | bytes 8650752 | tf_op jit(solution)/shard_map/transpose | solution.py:268
  815.9 1.3 convert_bitcast_fusion
  817.2 1.6 copy.84
  818.9 1.9 copy.85
  820.7 41.9 %reduce-scatter.7.cloned.1.call-done = bf16[12,256,128]{2,1,0:T(8,128)(2,1)} async-done(((bf16[96,256,128]{2,1,0:T(8,128)(2,1)}), bf16[12,256,128]{2,1,0:T(8,128)(2,1)}) %reduce-scatter.7.cloned.1.call-update) | async-done | bytes 786448 | tf_op jit(solution)/shard_map/reduce_scatter | solution.py:261
  862.7 1.4 copy.83
  864.1 1.2 copy.89
  865.2 1.3 fusion
  866.5 22.1 %reduce-scatter.11.cloned.1.call-done = bf16[64,1536]{1,0:T(8,128)(2,1)} async-done(((bf16[256,1536]{1,0:T(8,128)(2,1)}), bf16[64,1536]{1,0:T(8,128)(2,1)}) %reduce-scatter.11.cloned.1.call-update) | async-done | bytes 196624 | tf_op jit(solution)/shard_map/reduce_scatter | solution.py:308
  (42 shorter events, 4.5 us)
Async XLA Ops:
  7.2 2.8 copy-start
  7.2 5.1 copy-start.1
  7.2 51.4 %all-gather.11.cloned.1.call-start = ((), (), s32[]{:S(2)}) async-start(), calls=%async_computation.5 | async-start | bytes 7077888 | tf_op jit(solution)/shard_map/all_gather | solution.py:156
  9.9 48.8 %copy-start.3 = (s32[48]{0:T(128)S(1)}, s32[48]{0:T(128)}, u32[]{:S(2)}) copy-start(s32[48]{0:T(128)} %count_ref.1) | copy-start | bytes 580
  9.9 135.2 %all-gather.17.cloned.1.call-start = ((), (), s32[]{:S(2)}) async-start(), calls=%async_computation.12 | async-start | bytes 1179648 | tf_op jit(solution)/shard_map/all_gather | solution.py:127
  12.2 135.0 %all-gather.15.cloned.1.call-start = ((), (), s32[]{:S(2)}) async-start(), calls=%async_computation.7 | async-start | bytes 7077888 | tf_op jit(solution)/shard_map/all_gather | solution.py:152
  13.7 183.1 %all-gather.13.cloned.1.call-start = ((), (), s32[]{:S(2)}) async-start(), calls=%async_computation.6 | async-start | bytes 7077888 | tf_op jit(solution)/shard_map/all_gather | solution.py:165
  58.6 357.8 %all-gather.19.cloned.1.call-start = ((), (), s32[]{:S(2)}) async-start(), calls=%async_computation.13 | async-start | bytes 15728640 | tf_op jit(solution)/shard_map/all_gather | solution.py:213
  196.9 508.9 %reduce-scatter.5.cloned.1.call-start = ((), (), s32[]{:S(2)}) async-start(), calls=%async_computation.8 | async-start | bytes 21626880 | tf_op jit(solution)/shard_map/reduce_scatter | solution.py:259
  416.5 315.8 %all-gather.21.cloned.1.call-start = ((), (), s32[]{:S(2)}) async-start(), calls=%async_computation.14 | async-start | bytes 1179648 | tf_op jit(solution)/shard_map/all_gather | solution.py:127
  417.2 398.7 %reduce-scatter.9.cloned.1.call-start = ((), (), s32[]{:S(2)}) async-start(), calls=%async_computation.10 | async-start | bytes 7077888 | tf_op jit(solution)/shard_map/reduce_scatter | solution.py:263
  705.8 29.3 %copy-start.2 = (bf16[256,256]{1,0:T(8,128)(2,1)S(1)}, bf16[256,256]{1,0:T(8,128)(2,1)}, u32[]{:S(2)}) copy-start(bf16[256,256]{1,0:T(8,128)(2,1)} %reduce_sum.24.latent_ref) | copy-start | bytes 393220
  705.8 156.9 %reduce-scatter.7.cloned.1.call-start = ((), (), s32[]{:S(2)}) async-start(), calls=%async_computation.9 | async-start | bytes 7077888 | tf_op jit(solution)/shard_map/reduce_scatter | solution.py:261
  706.5 182.1 %reduce-scatter.11.cloned.1.call-start = ((), (), s32[]{:S(2)}) async-start(), calls=%async_computation.11 | async-start | bytes 983040 | tf_op jit(solution)/shard_map/reduce_scatter | solution.py:308
Sparse Core Ops, SparseCore 0:
  10.5 48.1 all-gather.10
  61.1 23.3 all-gather.16
  86.9 45.3 all-gather.14
  134.7 45.3 all-gather.12
  197.0 219.4 all-gather.18
  418.7 286.9 reduce-scatter.4
  708.2 24.0 all-gather.20
  735.7 61.7 reduce-scatter.8
  800.9 61.7 reduce-scatter.6
  865.4 23.1 reduce-scatter.10
